TPU v7x, 128 devices: a whole 4x4x4 slice. The times are simulated.
128 devices in a mesh: tok: 8 (over z, x_lo), head: 16 (over x_hi, y, core).
Axes of the slice: x: 4 (x_hi: 2, x_lo: 2; x = x_hi * 2 + x_lo), y: 4, z: 4, core: 2. Of those that a mesh axis runs over, the one named last changes fastest.
Arguments:
- block_states: bfloat16 [2048, 4096], P('tok', 'head'), may hold values from -24 to 24
- token_ids: int32 [2048], replicated, may hold values from 0 to 100351
- accept: int32 [2048], P('tok'), may hold values 0 or 1
- cache_lengths: int32 [8], replicated, may hold values from 1 to 5120, as said below
- cache_keys: bfloat16 [8192, 4096], P('tok', 'head'), may hold values from -300 to 300
- cache_values: bfloat16 [8192, 4096], P('tok', 'head'), may hold values from -6 to 6
- w_query: bfloat16 [4096, 4096], P(None, 'head'), may hold values from -0.09375 to 0.09375
- w_key: bfloat16 [4096, 4096], P(None, 'head'), may hold values from -0.09375 to 0.09375
- w_value: bfloat16 [4096, 4096], P(None, 'head'), may hold values from -0.09375 to 0.09375
- w_out: bfloat16 [4096, 4096], P('head'), may hold values from -0.09375 to 0.09375
- attn_gain: float32 [4096], replicated, may hold values from 0.25 to 1.75
- final_gain: float32 [4096], replicated, may hold values from 0.25 to 1.75
- embed: bfloat16 [100352, 4096], P('tok', 'head'), may hold values from -6 to 6
- lm_head: bfloat16 [100352, 4096], P(('tok', 'head')), may hold values from -0.25 to 0.25
Outputs:
- hiddens: bfloat16 [2048, 4096], P(('tok', 'head'))
- request_norms: float32 [8], replicated
- top_logits: float32 [2048], replicated
Inputs may be any that keep to these rules, and one draw needn't show every extreme that they name: `cache_lengths`: each request has 1 or more cached positions; the counts sum to 8192 and the largest is exactly 5120.
All inputs are finite; a program needn't handle non-finite values. No bound on the sum of `accept` on one device may be relied on, other than what follows from the above.
Results may differ from a plain program's by a relative error of at most 0.0068.
Values may be sent and summed in bfloat16 or wider, within the bound.
A program may use at most 192 MiB of HBM per device.

v0:
```python
import math
import jax
import jax.numpy as jnp
from jax import lax
from jax.sharding import PartitionSpec as P

HEAD_DIM = 128
EPSILON = 1e-06


def row_norm(values):
    return values * lax.rsqrt(jnp.mean(values * values, axis=-1, keepdims=True) + EPSILON)


def softmax_block(softmax_state, query_heads, key_block, value_block, valid_keys, score_scale):
    running_max, running_sum, running_acc = softmax_state
    scores = (
        jnp.einsum("qhd,khd->hqk", query_heads, key_block, preferred_element_type=jnp.float32)
        * score_scale
    )
    masked = jnp.where(valid_keys[None, None, :], scores, -1e30)
    new_max = jnp.maximum(running_max, jnp.max(masked, axis=-1))
    weights = jnp.where(valid_keys[None, None, :], jnp.exp(masked - new_max[:, :, None]), 0.0)
    factor = jnp.exp(running_max - new_max)
    running_sum = running_sum * factor + jnp.sum(weights, axis=-1)
    running_acc = running_acc * factor[:, :, None] + jnp.einsum(
        "hqk,khd->hqd", weights, value_block.astype(jnp.float32)
    )
    return (new_max, running_sum, running_acc)


def shards(
    block_states,
    token_ids,
    accept,
    cache_lengths,
    cache_keys,
    cache_values,
    w_query,
    w_key,
    w_value,
    w_out,
    attn_gain,
    final_gain,
    embed,
    lm_head,
):
    tok_index = lax.axis_index("tok")
    head_index = lax.axis_index("head")
    tok_count = lax.axis_size("tok")
    head_count = lax.axis_size("head")
    block_rows = block_states.shape[0]
    model_width = w_query.shape[0]
    local_width = w_query.shape[1]
    heads_here = local_width // HEAD_DIM
    share_rows = block_rows // head_count
    key_span = 512
    score_scale = 1.0 / math.sqrt(HEAD_DIM)
    offsets = jnp.cumsum(cache_lengths) - cache_lengths
    zero_rows = jnp.zeros((key_span, local_width), jnp.bfloat16)
    gathered_keys, gathered_values = (
        lax.all_gather(cache_keys, "tok", axis=0, tiled=True),
        lax.all_gather(cache_values, "tok", axis=0, tiled=True),
    )
    gathered_keys = jnp.concatenate([gathered_keys, zero_rows], axis=0)
    gathered_values = jnp.concatenate([gathered_values, zero_rows], axis=0)

    def attention(queries, key_rows, value_rows):
        query_heads = queries.reshape(block_rows, heads_here, HEAD_DIM)
        own_state = softmax_block(
            (
                jnp.full((heads_here, block_rows), -1e30, jnp.float32),
                jnp.zeros((heads_here, block_rows), jnp.float32),
                jnp.zeros((heads_here, block_rows, HEAD_DIM), jnp.float32),
            ),
            query_heads,
            key_rows.reshape(block_rows, heads_here, HEAD_DIM),
            value_rows.reshape(block_rows, heads_here, HEAD_DIM),
            jnp.ones((block_rows,), bool),
            score_scale,
        )
        request_begin = offsets[tok_index]
        request_length = cache_lengths[tok_index]
        block_count = (request_length + key_span - 1) // key_span

        def advance(turn_index, softmax_state):
            key_start = request_begin + turn_index * key_span
            key_block = lax.dynamic_slice_in_dim(gathered_keys, key_start, key_span, 0).reshape(
                key_span, heads_here, HEAD_DIM
            )
            value_block = lax.dynamic_slice_in_dim(gathered_values, key_start, key_span, 0).reshape(
                key_span, heads_here, HEAD_DIM
            )
            valid_keys = (
                turn_index * key_span + jnp.arange(key_span, dtype=jnp.int32) < request_length
            )
            return softmax_block(
                softmax_state, query_heads, key_block, value_block, valid_keys, score_scale
            )

        final_state = lax.fori_loop(0, block_count, advance, own_state)
        running_max, running_sum, running_acc = final_state
        result = running_acc / running_sum[:, :, None]
        return (
            jnp.transpose(result, (1, 0, 2)).reshape(block_rows, local_width).astype(jnp.bfloat16)
        )

    def run_layer(features):
        piece_cols = lax.all_gather(features, "head", axis=1, tiled=True)
        query_acc = jnp.dot(piece_cols, w_query, preferred_element_type=jnp.float32)
        key_acc = jnp.dot(piece_cols, w_key, preferred_element_type=jnp.float32)
        value_acc = jnp.dot(piece_cols, w_value, preferred_element_type=jnp.float32)
        own_rows = lax.dynamic_slice_in_dim(piece_cols, head_index * share_rows, share_rows, 0)
        residual = own_rows
        query_acc, key_acc, value_acc, residual = (query_acc, key_acc, value_acc, residual)
        attended = attention(
            query_acc.astype(jnp.bfloat16),
            key_acc.astype(jnp.bfloat16),
            value_acc.astype(jnp.bfloat16),
        )
        projected = lax.psum_scatter(
            jnp.dot(attended, w_out, preferred_element_type=jnp.float32),
            "head",
            scatter_dimension=0,
            tiled=True,
        )
        return (residual.astype(jnp.float32) + row_norm(projected) * attn_gain).astype(jnp.bfloat16)

    first_pass = run_layer(block_states)
    row_piece = lax.all_gather(first_pass, ("tok", "head"), axis=0, tiled=True)
    piece_rows = row_piece.shape[0]
    widened = row_piece.astype(jnp.float32)
    row_squares = jnp.sum(widened * widened, axis=-1)
    normed = (row_norm(widened) * final_gain).astype(jnp.bfloat16)
    logits = lax.dot_general(
        normed, lm_head, (((1,), (1,)), ((), ())), preferred_element_type=jnp.float32
    )
    best = jnp.max(logits, axis=1)
    owners = jnp.arange(piece_rows, dtype=jnp.int32) // block_rows
    one_hot = (owners[:, None] == jnp.arange(tok_count, dtype=jnp.int32)[None, :]).astype(
        jnp.float32
    )
    square_sums = jnp.dot(row_squares, one_hot, precision=lax.Precision.HIGHEST)
    top_local, square_sums = (best, square_sums)
    top_logits = lax.pmax(top_local, ("tok", "head"))
    request_norms = jnp.sqrt(square_sums / (block_rows * model_width))
    vocab_here = embed.shape[0]
    local_ids = token_ids - tok_index * vocab_here
    inside_vocab = (local_ids >= 0) & (local_ids < vocab_here)
    looked_up = jnp.take(embed, jnp.clip(local_ids, 0, vocab_here - 1), axis=0)
    looked_up = jnp.where(inside_vocab[:, None], looked_up, jnp.zeros_like(looked_up)).astype(
        jnp.float32
    )
    embedded = lax.psum_scatter(
        looked_up.astype(jnp.bfloat16), "tok", scatter_dimension=0, tiled=True
    )
    swapped = jnp.where((accept == 1)[:, None], embedded, block_states)
    hiddens = run_layer(swapped)
    return (hiddens, request_norms, top_logits)


def solution(mesh):
    placed = (
        P("tok", "head"),
        P(),
        P("tok"),
        P(),
        P("tok", "head"),
        P("tok", "head"),
        P(None, "head"),
        P(None, "head"),
        P(None, "head"),
        P("head", None),
        P(),
        P(),
        P("tok", "head"),
        P(("tok", "head"), None),
    )
    return jax.shard_map(
        shards,
        mesh=mesh,
        in_specs=placed,
        out_specs=(P(("tok", "head"), None), P(), P()),
        check_vma=False,
    )
```

profile of v0, /device:TPU:1, one launch (start us, length us, event | category | flops | bytes accessed | tf_op | source)
XLA Modules:
  0.0 832.7 jit_solution(10681744635398324091)
XLA Ops:
  9.6 10.3 %gather_fusion = bf16[2048,256]{1,0:T(8,128)(2,1)S(1)} fusion(bf16[12544,256]{1,0:T(8,128)(2,1)} %param.30, s32[2048]{0:T(1024)S(1)} %fusion.34), kind=kCustom, calls=%fused_computation | custom fusion | bytes 2105344 | tf_op jit(solution)/shard_map/jit(_take)/gather | solution.py:150
  19.9 2.4 select_select_fusion
  23.1 39.3 %reduce-scatter.4.cloned.1.call-done = bf16[256,256]{1,0:T(8,128)(2,1)} async-done(((bf16[2048,256]{1,0:T(8,128)(2,1)}), bf16[256,256]{1,0:T(8,128)(2,1)}) %reduce-scatter.4.cloned.1.call-update) | async-done | bytes 131088 | tf_op jit(solution)/shard_map/reduce_scatter | solution.py:154
  62.4 1.7 broadcast_select_fusion
  64.1 2.0 copy.39
  69.4 7.6 all-gather.12.cloned.1.call-done
  77.0 3.1 convolution_convert_fusion.2
  80.3 3.3 convolution_convert_fusion.1
  85.3 39.0 %all-gather.6.cloned.1.call-done = bf16[256,4096]{1,0:T(8,128)(2,1)} async-done(((bf16[256,256]{1,0:T(8,128)(2,1)}), bf16[256,4096]{1,0:T(8,128)(2,1)}) %all-gather.6.cloned.1.call-update) | async-done | bytes 2097168 | tf_op jit(solution)/shard_map/all_gather | solution.py:109
  124.3 3.3 convolution_convert_fusion.5
  129.0 85.2 %all-gather.8.cloned.1.call-done = bf16[8192,256]{0,1:T(8,128)(2,1)} async-done(((bf16[1024,256]{0,1:T(8,128)(2,1)}), bf16[8192,256]{0,1:T(8,128)(2,1)}) %all-gather.8.cloned.1.call-update) | async-done | bytes 4194320 | tf_op jit(solution)/shard_map/all_gather | solution.py:62
  214.2 4.6 concatenate.6
  218.8 87.8 %all-gather.10.cloned.1.call-done = bf16[8192,256]{0,1:T(8,128)(2,1)} async-done(((bf16[1024,256]{0,1:T(8,128)(2,1)}), bf16[8192,256]{0,1:T(8,128)(2,1)}) %all-gather.10.cloned.1.call-update) | async-done | bytes 4194320 | tf_op jit(solution)/shard_map/all_gather | solution.py:63
  306.6 4.6 concatenate.7
  311.2 3.8 while.29
  311.8 1.3 constant_dynamic-slice_fusion.7
  315.2 2.7 fusion.42
  318.4 3.1 convolution_convert_fusion.3
  321.9 3.8 while.28
  322.5 1.3 constant_dynamic-slice_fusion.6
  325.9 2.7 fusion.41
  328.6 102.6 %reduce-scatter.8.cloned.1.call-done = f32[16,4096]{1,0:T(8,128)} async-done(((f32[256,4096]{1,0:T(8,128)}), f32[16,4096]{1,0:T(8,128)}) %reduce-scatter.8.cloned.1.call-update) | async-done | bytes 262160 | tf_op jit(solution)/shard_map/reduce_scatter | solution.py:121
  431.2 1.1 multiply_reduce_fusion
  432.3 82.7 %reduce-scatter.6.cloned.1.call-done = f32[16,4096]{1,0:T(8,128)} async-done(((f32[256,4096]{1,0:T(8,128)}), f32[16,4096]{1,0:T(8,128)}) %reduce-scatter.6.cloned.1.call-update) | async-done | bytes 262160 | tf_op jit(solution)/shard_map/reduce_scatter | solution.py:121
  515.1 1.1 multiply_reduce_fusion.1
  516.2 2.0 add_convert_fusion
  518.2 214.2 %all-gather.14.cloned.1.call-done = bf16[2048,4096]{1,0:T(8,128)(2,1)} async-done(((bf16[16,4096]{1,0:T(8,128)(2,1)}), bf16[2048,4096]{1,0:T(8,128)(2,1)}) %all-gather.14.cloned.1.call-update) | async-done | bytes 16777232 | tf_op jit(solution)/shard_map/all_gather | solution.py:130
  732.4 7.5 fusion.14
  740.0 3.1 copy-done.4
  743.1 17.2 %fusion.21 = f32[2048]{0:T(1024)S(1)} fusion(bf16[784,4096]{1,0:T(8,128)(2,1)} %param.31, bf16[2048,4096]{1,0:T(8,128)(2,1)S(1)} %copy-done.4, f32[4096]{0:T(1024)S(1)} %copy-done.10, f32[2048]{0:T(1024)S(1)} %add_rsqrt_fusion), kind=kOutput, calls=%fused_computation.39 | convolution fusion | flops 13188495360 | bytes 23232512 | tf_op jit(solution)/shard_map/dot_general | solution.py:135
  760.3 63.8 %pmax.7 = f32[2048]{0:T(1024)} all-reduce(f32[2048]{0:T(1024)S(1)} %fusion.21), channel_id=1, replica_groups=mesh['tok'=8,'head'=16] {'tok','head'}, use_global_device_ids=true, to_apply=%region_20.21 | all-reduce | flops 2048 | bytes 16384 | tf_op jit(solution)/shard_map/pmax | solution.py:145
  824.1 1.1 fusion.25
  (85 shorter events, 12.8 us)
Async XLA Ops:
  8.0 307.2 %copy-start = (bf16[256,4096]{1,0:T(8,128)(2,1)S(1)}, bf16[256,4096]{1,0:T(8,128)(2,1)}, u32[]{:S(2)}) copy-start(bf16[256,4096]{1,0:T(8,128)(2,1)} %param.27) | copy-start | bytes 6291460
  8.0 54.4 %reduce-scatter.4.cloned.1.call-start = ((), (), s32[]{:S(2)}) async-start(), calls=%async_computation.3 | async-start | bytes 1179648 | tf_op jit(solution)/shard_map/reduce_scatter | solution.py:154
  19.9 3.1 copy-start.11
  19.9 42.4 %copy-start.8 = (bf16[256,256]{1,0:T(8,128)(2,1)S(1)}, bf16[256,256]{1,0:T(8,128)(2,1)}, u32[]{:S(2)}) copy-start(bf16[256,256]{1,0:T(8,128)(2,1)} %param.18) | copy-start | bytes 393220
  22.4 43.9 %copy-start.7 = (bf16[1024,256]{1,0:T(8,128)(2,1)S(1)}, bf16[1024,256]{1,0:T(8,128)(2,1)}, u32[]{:S(2)}) copy-start(bf16[1024,256]{1,0:T(8,128)(2,1)} %param.23) | copy-start | bytes 1572868
  22.4 44.9 %copy-start.12 = (s32[8]{0:T(128)S(1)}, s32[8]{0:T(128)}, u32[]{:S(2)}) copy-start(s32[8]{0:T(128)} %param.21) | copy-start | bytes 100
  22.4 54.6 %all-gather.12.cloned.1.call-start = ((), (), s32[]{:S(2)}) async-start(), calls=%async_computation.8 | async-start | bytes 2228224 | tf_op jit(solution)/shard_map/all_gather | solution.py:109
  23.0 101.3 %all-gather.6.cloned.1.call-start = ((), (), s32[]{:S(2)}) async-start(), calls=%async_computation.4 | async-start | bytes 2228224 | tf_op jit(solution)/shard_map/all_gather | solution.py:109
  64.1 150.1 %all-gather.8.cloned.1.call-start = ((), (), s32[]{:S(2)}) async-start(), calls=%async_computation.5 | async-start | bytes 4718592 | tf_op jit(solution)/shard_map/all_gather | solution.py:62
  66.2 240.4 %all-gather.10.cloned.1.call-start = ((), (), s32[]{:S(2)}) async-start(), calls=%async_computation.6 | async-start | bytes 4718592 | tf_op jit(solution)/shard_map/all_gather | solution.py:63
  67.3 364.0 %reduce-scatter.8.cloned.1.call-start = ((), (), s32[]{:S(2)}) async-start(), calls=%async_computation.9 | async-start | bytes 4456448 | tf_op jit(solution)/shard_map/reduce_scatter | solution.py:121
  80.3 3.7 copy-start.2
  80.3 3.7 copy-start.6
  124.3 3.3 copy-start.3
  124.3 3.5 copy-start.5
  318.0 197.1 %reduce-scatter.6.cloned.1.call-start = ((), (), s32[]{:S(2)}) async-start(), calls=%async_computation.7 | async-start | bytes 4456448 | tf_op jit(solution)/shard_map/reduce_scatter | solution.py:121
  328.6 187.6 %copy-start.9 = (f32[4096]{0:T(1024)S(1)}, f32[4096]{0:T(1024)}, u32[]{:S(2)}) copy-start(f32[4096]{0:T(1024)} %param.28) | copy-start | bytes 49156
  328.6 403.8 %all-gather.14.cloned.1.call-start = ((), (), s32[]{:S(2)}) async-start(), calls=%async_computation.10 | async-start | bytes 16908288 | tf_op jit(solution)/shard_map/all_gather | solution.py:130
  518.2 221.8 %copy-start.10 = (f32[4096]{0:T(1024)S(1)}, f32[4096]{0:T(1024)}, u32[]{:S(2)}) copy-start(f32[4096]{0:T(1024)} %param.29) | copy-start | bytes 49156
  732.4 10.7 %copy-start.4 = (bf16[2048,4096]{1,0:T(8,128)(2,1)S(1)}, bf16[2048,4096]{1,0:T(8,128)(2,1)}, u32[]{:S(2)}) copy-start(bf16[2048,4096]{1,0:T(8,128)(2,1)} %all-gather.14.cloned.1.call-done) | copy-start | bytes 50331652
  743.1 82.2 %copy-start.1 = (bf16[256,4096]{1,0:T(8,128)(2,1)S(1)}, bf16[256,4096]{1,0:T(8,128)(2,1)}, u32[]{:S(2)}) copy-start(bf16[256,4096]{1,0:T(8,128)(2,1)} %param.27) | copy-start | bytes 6291460
Sparse Core Ops, SparseCore 0:
  22.5 39.8 reduce-scatter.3
  518.3 214.0 all-gather.13
Sparse Core Ops, SparseCore 1:
  25.2 51.8 all-gather.11
  79.7 44.5 all-gather.5
  125.8 88.3 all-gather.7
  215.9 90.7 all-gather.9
  318.0 113.1 reduce-scatter.7
  435.8 79.2 reduce-scatter.5
where the time goes:
time: 834 us; the launch traced here: 833 us
  waiting for transfers between devices  659 us (79%)
  blocking collectives  63.8 us (8%)
  matrix products  41.5 us (5%)
  local copies, waits for them, and re-layouts  30.3 us (4%)
  other arithmetic  19.6 us (2%)
  between operations  16.6 us (2%)
    all_gather x1, waiting for transfers between devices, shards(): row_piece = lax.all_gather(first_pass, ('tok', 'head'), axis=0, tiled=True)  214 us
    reduce_scatter x2, waiting for transfers between devices, run_layer(): lax.psum_scatter(jnp.dot(attended, w_out, preferred_element_type=jnp.floa...  185 us
    all_gather x1, waiting for transfers between devices, shards(): lax.all_gather(cache_values, 'tok', axis=0, tiled=True)  87.8 us
    all_gather x1, waiting for transfers between devices, shards(): lax.all_gather(cache_keys, 'tok', axis=0, tiled=True)  85.2 us
    pmax x1, blocking collectives, shards(): top_logits = lax.pmax(top_local, ('tok', 'head'))  63.8 us
    all_gather x2, waiting for transfers between devices, run_layer(): piece_cols = lax.all_gather(features, 'head', axis=1, tiled=True)  46.6 us
    reduce_scatter x1, waiting for transfers between devices, shards(): lax.psum_scatter(looked_up.astype(jnp.bfloat16), 'tok', scatter_dimension...  39.3 us
    dot_general x1, matrix products, shards(): lax.dot_general(normed, lm_head, (((1,), (1,)), ((), ())), preferred_elem...  17.2 us
  transfers between devices with their start and end apart: 8, of which 8 were waited for; matrix products, arithmetic and copies ran while one was open for 4% of the time, Pallas kernels for 0%

commit v1 on v0

--- a/solution.py
+++ b/solution.py
@@ -6,6 +6,16 @@
 
 HEAD_DIM = 128
 EPSILON = 1e-06
+
+
+def _cut_keys(state, chip_axis):
+    b_next = jnp.concatenate(
+        lax.all_to_all(
+            jnp.stack([state for _ in range(lax.axis_size(chip_axis))], axis=0), chip_axis, 0, 0
+        ),
+        axis=0,
+    )
+    return b_next
 
 
 def row_norm(values):
@@ -60,7 +70,7 @@
     zero_rows = jnp.zeros((key_span, local_width), jnp.bfloat16)
     gathered_keys, gathered_values = (
         lax.all_gather(cache_keys, "tok", axis=0, tiled=True),
-        lax.all_gather(cache_values, "tok", axis=0, tiled=True),
+        _cut_keys(cache_values, "tok"),
     )
     gathered_keys = jnp.concatenate([gathered_keys, zero_rows], axis=0)
     gathered_values = jnp.concatenate([gathered_values, zero_rows], axis=0)

time: 834 us -> 746 us (0.89)
  waiting for transfers between devices: 659 us -> 552 us
  local copies, waits for them, and re-layouts: 30.3 us -> 44.9 us
    all_gather x1 -> x0, waiting for transfers between devices: 87.8 us -> none  [shards(): lax.all_gather(cache_values, 'tok', axis=0, tiled=True)]
    all_gather x2, waiting for transfers between devices: 46.6 us -> 0.03 us  [run_layer(): piece_cols = lax.all_gather(features, 'head', axis=1, tiled=True)]
    all_to_all x0 -> x1, waiting for transfers between devices: none -> 39.5 us  [_cut_keys(): lax.all_to_all(jnp.stack([state for _ in range(lax.axis_size(chip_axis))]...]
    all_gather x1, waiting for transfers between devices: 85.2 us -> 73.4 us  [shards(): lax.all_gather(cache_keys, 'tok', axis=0, tiled=True)]
  transfers between devices with their start and end apart: 8 -> 8, of which waited for: 8 -> 6; matrix products, arithmetic and copies ran while one was open for 4% -> 7% of each run, Pallas kernels for 0% -> 0%
where the time goes in v1:
time: 746 us; the launch traced here: 745 us
  waiting for transfers between devices  552 us (74%)
  blocking collectives  63.8 us (9%)
  local copies, waits for them, and re-layouts  44.9 us (6%)
  matrix products  41.7 us (6%)
  other arithmetic  19.6 us (3%)
  between operations  16.7 us (2%)
    all_gather x1, waiting for transfers between devices, shards(): row_piece = lax.all_gather(first_pass, ('tok', 'head'), axis=0, tiled=True)  214 us
    reduce_scatter x2, waiting for transfers between devices, run_layer(): lax.psum_scatter(jnp.dot(attended, w_out, preferred_element_type=jnp.floa...  185 us
    all_gather x1, waiting for transfers between devices, shards(): lax.all_gather(cache_keys, 'tok', axis=0, tiled=True)  73.4 us
    pmax x1, blocking collectives, shards(): top_logits = lax.pmax(top_local, ('tok', 'head'))  63.8 us
    all_to_all x1, waiting for transfers between devices, _cut_keys(): lax.all_to_all(jnp.stack([state for _ in range(lax.axis_size(chip_axis))]...  39.5 us
    reduce_scatter x1, waiting for transfers between devices, shards(): lax.psum_scatter(looked_up.astype(jnp.bfloat16), 'tok', scatter_dimension...  39.3 us
    dot_general x1, matrix products, shards(): lax.dot_general(normed, lm_head, (((1,), (1,)), ((), ())), preferred_elem...  17.2 us
  transfers between devices with their start and end apart: 8, of which 6 were waited for; matrix products, arithmetic and copies ran while one was open for 7% of the time, Pallas kernels for 0%

profile of v1, /device:TPU:1, one launch (start us, length us, event | category | flops | bytes accessed | tf_op | source)
XLA Modules:
  0.0 744.8 jit_solution(68889332668762787)
XLA Ops:
  9.6 10.3 %gather_fusion = bf16[2048,256]{1,0:T(8,128)(2,1)S(1)} fusion(bf16[12544,256]{1,0:T(8,128)(2,1)} %param.30, s32[2048]{0:T(1024)S(1)} %fusion.34), kind=kCustom, calls=%fused_computation | custom fusion | bytes 2105344 | tf_op jit(solution)/shard_map/jit(_take)/gather | solution.py:160
  19.9 2.4 select_select_fusion
  23.1 39.3 %reduce-scatter.4.cloned.1.call-done = bf16[256,256]{1,0:T(8,128)(2,1)} async-done(((bf16[2048,256]{1,0:T(8,128)(2,1)}), bf16[256,256]{1,0:T(8,128)(2,1)}) %reduce-scatter.4.cloned.1.call-update) | async-done | bytes 131088 | tf_op jit(solution)/shard_map/reduce_scatter | solution.py:164
  62.4 1.7 broadcast_select_fusion
  64.1 2.1 copy.79
  66.4 2.5 stack.2
  68.9 4.7 all-to-all-start
  75.7 39.5 %all-to-all-done = bf16[8,1024,256]{1,2,0:T(8,128)(2,1)} async-done(((bf16[8,1024,256]{1,2,0:T(8,128)(2,1)}), bf16[8,1024,256]{1,2,0:T(8,128)(2,1)}, u32[]{:S(2)}, u32[]{:S(2)}) %all-to-all-start) | async-done | bytes 4194336 | tf_op jit(solution)/shard_map/all_to_all | solution.py:13
  115.2 6.4 copy.81
  121.6 6.4 copy.106
  128.0 4.7 concatenate.7.clone
  132.7 3.1 convolution_convert_fusion.2
  136.0 3.5 convolution_convert_fusion.1
  141.3 3.3 convolution_convert_fusion.5
  146.0 73.4 %all-gather.7.cloned.1.call-done = bf16[8192,256]{0,1:T(8,128)(2,1)} async-done(((bf16[1024,256]{0,1:T(8,128)(2,1)}), bf16[8192,256]{0,1:T(8,128)(2,1)}) %all-gather.7.cloned.1.call-update) | async-done | bytes 4194320 | tf_op jit(solution)/shard_map/all_gather | solution.py:72
  219.4 4.6 concatenate.6
  224.0 3.7 while.29
  224.5 1.3 constant_dynamic-slice_fusion.7
  227.9 2.7 fusion.42
  231.1 3.1 convolution_convert_fusion.3
  234.6 3.7 while.28
  235.2 1.3 constant_dynamic-slice_fusion.6
  238.5 2.7 fusion.41
  241.2 102.0 %reduce-scatter.8.cloned.1.call-done = f32[16,4096]{1,0:T(8,128)} async-done(((f32[256,4096]{1,0:T(8,128)}), f32[16,4096]{1,0:T(8,128)}) %reduce-scatter.8.cloned.1.call-update) | async-done | bytes 262160 | tf_op jit(solution)/shard_map/reduce_scatter | solution.py:131
  344.4 82.8 %reduce-scatter.6.cloned.1.call-done = f32[16,4096]{1,0:T(8,128)} async-done(((f32[256,4096]{1,0:T(8,128)}), f32[16,4096]{1,0:T(8,128)}) %reduce-scatter.6.cloned.1.call-update) | async-done | bytes 262160 | tf_op jit(solution)/shard_map/reduce_scatter | solution.py:131
  428.2 2.0 add_convert_fusion
  430.3 214.2 %all-gather.11.cloned.1.call-done = bf16[2048,4096]{1,0:T(8,128)(2,1)} async-done(((bf16[16,4096]{1,0:T(8,128)(2,1)}), bf16[2048,4096]{1,0:T(8,128)(2,1)}) %all-gather.11.cloned.1.call-update) | async-done | bytes 16777232 | tf_op jit(solution)/shard_map/all_gather | solution.py:140
  644.4 7.5 %fusion.14 = f32[2048]{0:T(1024)S(1)} fusion(bf16[2048,4096]{1,0:T(8,128)(2,1)} %all-gather.11.cloned.1.call-done), kind=kLoop, calls=%fused_computation.33 | loop fusion | flops 25163776 | bytes 16785408 | tf_op jit(solution)/shard_map/reduce_sum | solution.py:143
  652.0 3.1 copy-done.4
  655.1 17.2 %fusion.21 = f32[2048]{0:T(1024)S(1)} fusion(bf16[784,4096]{1,0:T(8,128)(2,1)} %param.31, bf16[2048,4096]{1,0:T(8,128)(2,1)S(1)} %copy-done.4, f32[4096]{0:T(1024)S(1)} %copy-done.10, f32[2048]{0:T(1024)S(1)} %add_rsqrt_fusion), kind=kOutput, calls=%fused_computation.39 | convolution fusion | flops 13188495360 | bytes 23232512 | tf_op jit(solution)/shard_map/dot_general | solution.py:145
  672.3 63.8 %pmax.7 = f32[2048]{0:T(1024)} all-reduce(f32[2048]{0:T(1024)S(1)} %fusion.21), channel_id=1, replica_groups=mesh['tok'=8,'head'=16] {'tok','head'}, use_global_device_ids=true, to_apply=%region_20.21 | all-reduce | flops 2048 | bytes 16384 | tf_op jit(solution)/shard_map/pmax | solution.py:155
  736.1 1.1 fusion.25
  (87 shorter events, 14.1 us)
Async XLA Ops:
  8.0 219.9 %copy-start = (bf16[256,4096]{1,0:T(8,128)(2,1)S(1)}, bf16[256,4096]{1,0:T(8,128)(2,1)}, u32[]{:S(2)}) copy-start(bf16[256,4096]{1,0:T(8,128)(2,1)} %param.27) | copy-start | bytes 6291460
  8.0 54.3 %reduce-scatter.4.cloned.1.call-start = ((), (), s32[]{:S(2)}) async-start(), calls=%async_computation.4 | async-start | bytes 1179648 | tf_op jit(solution)/shard_map/reduce_scatter | solution.py:164
  19.9 3.1 copy-start.11
  19.9 42.4 %copy-start.8 = (bf16[256,256]{1,0:T(8,128)(2,1)S(1)}, bf16[256,256]{1,0:T(8,128)(2,1)}, u32[]{:S(2)}) copy-start(bf16[256,256]{1,0:T(8,128)(2,1)} %param.18) | copy-start | bytes 393220
  22.4 43.8 %copy-start.7 = (bf16[1024,256]{1,0:T(8,128)(2,1)S(1)}, bf16[1024,256]{1,0:T(8,128)(2,1)}, u32[]{:S(2)}) copy-start(bf16[1024,256]{1,0:T(8,128)(2,1)} %param.23) | copy-start | bytes 1572868
  22.4 110.3 %all-gather.9.cloned.1.call-start = ((), (), s32[]{:S(2)}) async-start(), calls=%async_computation.8 | async-start | bytes 2228224 | tf_op jit(solution)/shard_map/all_gather | solution.py:119
  23.0 118.3 %all-gather.5.cloned.1.call-start = ((), (), s32[]{:S(2)}) async-start(), calls=%async_computation.5 | async-start | bytes 2228224 | tf_op jit(solution)/shard_map/all_gather | solution.py:119
  64.0 155.3 %all-gather.7.cloned.1.call-start = ((), (), s32[]{:S(2)}) async-start(), calls=%async_computation.6 | async-start | bytes 4718592 | tf_op jit(solution)/shard_map/all_gather | solution.py:72
  68.9 4.7 copy-start.12
  68.9 46.2 %all-to-all-start = ((bf16[8,1024,256]{1,2,0:T(8,128)(2,1)}), bf16[8,1024,256]{1,2,0:T(8,128)(2,1)}, u32[]{:S(2)}, u32[]{:S(2)}) async-start(bf16[8,1024,256]{1,2,0:T(8,128)(2,1)} %stack.2), calls=%async_computation.1 | async-start | bytes 8388608 | tf_op jit(solution)/shard_map/all_to_all | solution.py:13
  73.6 269.6 %reduce-scatter.8.cloned.1.call-start = ((), (), s32[]{:S(2)}) async-start(), calls=%async_computation.9 | async-start | bytes 4456448 | tf_op jit(solution)/shard_map/reduce_scatter | solution.py:131
  136.0 3.9 copy-start.2
  136.0 3.9 copy-start.6
  141.2 3.3 copy-start.3
  141.3 3.5 copy-start.5
  230.6 196.5 %reduce-scatter.6.cloned.1.call-start = ((), (), s32[]{:S(2)}) async-start(), calls=%async_computation.7 | async-start | bytes 4456448 | tf_op jit(solution)/shard_map/reduce_scatter | solution.py:131
  241.2 187.1 %copy-start.9 = (f32[4096]{0:T(1024)S(1)}, f32[4096]{0:T(1024)}, u32[]{:S(2)}) copy-start(f32[4096]{0:T(1024)} %param.28) | copy-start | bytes 49156
  241.2 403.2 %all-gather.11.cloned.1.call-start = ((), (), s32[]{:S(2)}) async-start(), calls=%async_computation.10 | async-start | bytes 16908288 | tf_op jit(solution)/shard_map/all_gather | solution.py:140
  430.2 221.7 %copy-start.10 = (f32[4096]{0:T(1024)S(1)}, f32[4096]{0:T(1024)}, u32[]{:S(2)}) copy-start(f32[4096]{0:T(1024)} %param.29) | copy-start | bytes 49156
  644.4 10.7 %copy-start.4 = (bf16[2048,4096]{1,0:T(8,128)(2,1)S(1)}, bf16[2048,4096]{1,0:T(8,128)(2,1)}, u32[]{:S(2)}) copy-start(bf16[2048,4096]{1,0:T(8,128)(2,1)} %all-gather.11.cloned.1.call-done) | copy-start | bytes 50331652
  655.1 82.2 %copy-start.1 = (bf16[256,4096]{1,0:T(8,128)(2,1)S(1)}, bf16[256,4096]{1,0:T(8,128)(2,1)}, u32[]{:S(2)}) copy-start(bf16[256,4096]{1,0:T(8,128)(2,1)} %param.27) | copy-start | bytes 6291460
Sparse Core Ops, SparseCore 0:
  22.5 39.7 reduce-scatter.3
  430.4 214.0 all-gather.10
Sparse Core Ops, SparseCore 1:
  25.1 51.7 all-gather.8
  79.7 50.7 all-gather.4
  131.9 87.4 all-gather.6
  230.7 112.5 reduce-scatter.7
  347.8 79.2 reduce-scatter.5
